TPU v7x, 32 devices: a whole 2x2x4 slice. The times are simulated.
32 devices in a mesh: seq: 8 (over z, x), head: 4 (over y, core).
Axes of the slice: x: 2, y: 2, z: 4, core: 2. Of those that a mesh axis runs over, the one named last changes fastest.
Arguments:
- queries: bfloat16 [9216, 32, 128], P(('seq', 'head')), may hold values from -4 to 4
- key_states: bfloat16 [9216, 4, 128], P(('seq', 'head')), may hold values from -4 to 4
- value_states: bfloat16 [9216, 4, 128], P(('seq', 'head')), may hold values from -6 to 6
- outputs: bfloat16 [9216, 32, 128], P(('seq', 'head')), may hold values from -6 to 6
- output_grad: bfloat16 [9216, 32, 128], P(('seq', 'head')), may hold values from -96 to 96
- logsumexp: float32 [9216, 32], P(('seq', 'head')), may hold values from 6.8 to 7.8
- random_owner: int32 [72, 3], replicated, may hold values from 0 to 7, all different within a row; in each aligned block of 9 rows (0 to 8, 9 to 17, ...) at most 4 rows name the same one
- random_slot: int32 [72, 3], replicated, may hold values from 0 to 8
Outputs:
- query_grad: bfloat16 [9216, 32, 128], P(('seq', 'head'))
- key_grad: bfloat16 [9216, 4, 128], P(('seq', 'head'))
- value_grad: bfloat16 [9216, 4, 128], P(('seq', 'head'))
Inputs may be any that keep to these rules, and one draw needn't show every extreme that they name: `random_owner`: each row names 3 different indices. Within the 9 rows of one index of seq (aligned blocks of 9 rows), no index of seq appears more than 4 times, and some index appears exactly 4 times in some block.
All inputs are finite; a program needn't handle non-finite values.
Results may differ from a plain program's by a relative error of at most 0.005.
Values may be sent and summed in bfloat16 or wider, within the bound.
A program may use at most 128 MiB of HBM per device.

v0:
```python
import jax
import jax.numpy as jnp
from jax import lax
from jax.sharding import PartitionSpec as P

HD = 128
BLK = 128
G = 2
RND = 3


def extended_2(value, sides, width):
    for axis, dim in sides:
        devices, length = (lax.axis_size(axis), value.shape[dim])
        up = [(i, (i + 1) % devices) for i in range(devices - 1)]
        down = [(j, i) for i, j in up]
        last = lax.slice_in_dim(value, length - width, length, axis=dim)
        leading = lax.slice_in_dim(value, 0, width, axis=dim)
        before = lax.ppermute(last, axis, up)
        after = lax.ppermute(leading, axis, down)
        value = jnp.concatenate([before, value, after], axis=dim)
    return value


def broadcast(value, axis, source):
    kept = jnp.where(lax.axis_index(axis) == source, value, 0).astype(value.dtype)
    return lax.psum(kept, axis)


def from_behind(value, axis, steps):
    count = lax.axis_size(axis)
    leading, last = (max(0, -steps), min(count, count - steps))
    return lax.ppermute(value, axis, [(source, source + steps) for source in range(leading, last)])


def block_grads(
    query_block, grad_block, logsum_block, delta_block, key_blocks, value_blocks, validity
):
    scaling = 1.0 / HD**0.5
    scores = (
        jnp.einsum("ighd,mjgd->mghij", query_block, key_blocks, preferred_element_type=jnp.float32)
        * scaling
    )
    weights = (
        jnp.exp(scores - jnp.transpose(logsum_block, (1, 2, 0))[None, :, :, :, None])
        * validity[:, None, None, None, None]
    )
    weights_rounded = weights.astype(jnp.bfloat16)
    weight_grad = jnp.einsum(
        "ighd,mjgd->mghij", grad_block, value_blocks, preferred_element_type=jnp.float32
    )
    score_grad = (
        weights * (weight_grad - jnp.transpose(delta_block, (1, 2, 0))[None, :, :, :, None])
    ).astype(jnp.bfloat16)
    query_part = (
        jnp.einsum("mghij,mjgd->ighd", score_grad, key_blocks, preferred_element_type=jnp.float32)
        * scaling
    )
    key_part = (
        jnp.einsum("mghij,ighd->mjgd", score_grad, query_block, preferred_element_type=jnp.float32)
        * scaling
    )
    value_part = jnp.einsum(
        "mghij,ighd->mjgd", weights_rounded, grad_block, preferred_element_type=jnp.float32
    )
    return (query_part, jnp.stack([key_part, value_part], axis=2))


def local_grads(query_split, grad_split, logsum_split, delta_split, chosen_kv, validity):

    def single_block(items):
        return block_grads(*items)

    return lax.map(
        single_block,
        (
            query_split,
            grad_split,
            logsum_split,
            delta_split,
            chosen_kv[:, :, :, 0],
            chosen_kv[:, :, :, 1],
            validity,
        ),
    )


def pair_lists(block_ids, owners, slots, blocks_local, block_count):
    window_ids = block_ids[:, None] + jnp.arange(-1, 2, dtype=jnp.int32)[None, :]
    random_ids = owners * blocks_local + slots
    window_ok = (window_ids >= G) & (window_ids <= block_count - 1)
    random_ok = (random_ids >= G) & (jnp.abs(random_ids - block_ids[:, None]) >= 2)
    validity = jnp.concatenate(
        [
            jnp.ones((block_ids.shape[0], G), jnp.float32),
            window_ok.astype(jnp.float32),
            random_ok.astype(jnp.float32),
        ],
        axis=1,
    )
    return (window_ids, random_ids, validity)


def per_device(
    queries, key_states, value_states, outputs, output_grad, logsumexp, random_owner, random_slot
):
    delta_seq = jnp.einsum("thd,thd->th", output_grad, outputs, preferred_element_type=jnp.float32)
    query_loc, key_loc, value_loc, grad_loc = (
        lax.all_to_all(queries, "head", split_axis=1, concat_axis=0, tiled=True),
        lax.all_to_all(key_states, "head", split_axis=1, concat_axis=0, tiled=True),
        lax.all_to_all(value_states, "head", split_axis=1, concat_axis=0, tiled=True),
        lax.all_to_all(output_grad, "head", split_axis=1, concat_axis=0, tiled=True),
    )
    logsum_loc, delta_loc = (
        lax.all_to_all(logsumexp, "head", split_axis=1, concat_axis=0, tiled=True),
        lax.all_to_all(delta_seq, "head", split_axis=1, concat_axis=0, tiled=True),
    )
    tok_count = query_loc.shape[0]
    heads_local = query_loc.shape[1]
    kv_heads = key_loc.shape[1]
    group = heads_local // kv_heads
    blocks_local = tok_count // BLK
    seq_count = lax.axis_size("seq")
    seq_index = lax.axis_index("seq")
    block_count = seq_count * blocks_local
    rows_each = blocks_local * RND
    most_slots = max(1, (rows_each + seq_count - 1) // seq_count)
    query_split = query_loc.reshape(blocks_local, BLK, kv_heads, group, HD)
    grad_split = grad_loc.reshape(blocks_local, BLK, kv_heads, group, HD)
    logsum_split = logsum_loc.reshape(blocks_local, BLK, kv_heads, group)
    delta_split = delta_loc.reshape(blocks_local, BLK, kv_heads, group)
    kv_loc = jnp.stack([key_loc, value_loc], axis=1)
    kv_blocks = kv_loc.reshape(blocks_local, BLK, 2, kv_heads, HD)
    block_ids = seq_index * blocks_local + jnp.arange(blocks_local, dtype=jnp.int32)
    my_owner = lax.dynamic_slice_in_dim(random_owner, seq_index * blocks_local, blocks_local, 0)
    my_slot = lax.dynamic_slice_in_dim(random_slot, seq_index * blocks_local, blocks_local, 0)
    window_ids, random_ids, validity = pair_lists(
        block_ids, my_owner, my_slot, blocks_local, block_count
    )
    owner_table = random_owner.reshape(seq_count, rows_each)
    slot_table = random_slot.reshape(seq_count, rows_each)
    entry_pos = jnp.arange(rows_each, dtype=jnp.int32)
    before_mask = entry_pos[None, :] < entry_pos[:, None]
    same_owner = owner_table[:, :, None] == owner_table[:, None, :]
    rank_table = jnp.sum((same_owner & before_mask[None, :, :]).astype(jnp.int32), axis=2)
    my_rank = lax.dynamic_slice_in_dim(rank_table, seq_index, 1, 0).reshape(blocks_local, RND)
    slot_ids = jnp.arange(most_slots, dtype=jnp.int32)
    local_ids = jnp.arange(blocks_local, dtype=jnp.int32)
    local_hits = (
        (owner_table == seq_index)[:, :, None, None]
        & (rank_table[:, :, None, None] == slot_ids[None, None, :, None])
        & (slot_table[:, :, None, None] == local_ids[None, None, None, :])
    )
    selector = jnp.sum(local_hits.astype(jnp.float32), axis=1)
    extended = extended_2(kv_loc, (("seq", 0),), BLK)
    ext_blocks = extended.reshape(blocks_local + 2, BLK, 2, kv_heads, HD)
    window_kv = jnp.stack(
        [ext_blocks[offset : offset + blocks_local] for offset in range(3)], axis=1
    )
    global_kv = broadcast(kv_loc[: G * BLK], "seq", 0).reshape(G, BLK, 2, kv_heads, HD)
    outgoing = jnp.einsum(
        "pml,lbtgd->pmbtgd",
        selector.astype(jnp.bfloat16),
        kv_blocks,
        preferred_element_type=jnp.float32,
    ).astype(jnp.bfloat16)
    fetched = lax.all_to_all(outgoing, "seq", split_axis=0, concat_axis=0, tiled=True)
    random_kv = fetched[my_owner, my_rank]
    global_wide = jnp.broadcast_to(global_kv[None], (blocks_local,) + global_kv.shape)
    chosen = jnp.concatenate([global_wide, window_kv, random_kv], axis=1)
    query_part, kv_part = local_grads(
        query_split, grad_split, logsum_split, delta_split, chosen, validity
    )
    global_part = jnp.sum(kv_part[:, :G], axis=0)
    window_part = kv_part[:, G : G + 3]
    random_part = kv_part[:, G + 3 :]
    global_total = lax.psum(global_part, "seq")
    padded_parts = [
        jnp.pad(window_part[:, offset], ((offset, 2 - offset), (0, 0), (0, 0), (0, 0), (0, 0)))
        for offset in range(3)
    ]
    ext_grad = padded_parts[0] + padded_parts[1] + padded_parts[2]
    own_grad = ext_grad[1 : blocks_local + 1]
    flat_target = (my_owner * most_slots + my_rank).reshape(-1)
    owner_onehot = (
        flat_target[None, :] == jnp.arange(seq_count * most_slots, dtype=jnp.int32)[:, None]
    ).astype(jnp.float32)
    returning = jnp.dot(
        owner_onehot,
        random_part.reshape(rows_each, -1),
        precision=lax.Precision.HIGHEST,
        preferred_element_type=jnp.float32,
    )
    returning = returning.reshape(seq_count, most_slots, BLK, 2, kv_heads, HD)
    from_upper = from_behind(ext_grad[0].astype(jnp.bfloat16), "seq", -1).astype(jnp.float32)
    from_lower = from_behind(ext_grad[blocks_local + 1].astype(jnp.bfloat16), "seq", 1).astype(
        jnp.float32
    )
    returned = lax.all_to_all(returning, "seq", split_axis=0, concat_axis=0, tiled=True)
    own_grad = own_grad.at[blocks_local - 1].add(from_upper)
    own_grad = own_grad.at[0].add(from_lower)
    own_grad = own_grad + jnp.einsum(
        "pml,pmbtgd->lbtgd",
        selector,
        returned,
        precision=lax.Precision.HIGHEST,
        preferred_element_type=jnp.float32,
    )
    global_here = jnp.where(seq_index == 0, global_total, jnp.zeros_like(global_total))
    own_grad = own_grad.at[:G].add(global_here)
    kv_grad = own_grad.reshape(tok_count, 2, kv_heads, HD)
    query_grad_loc = query_part.reshape(tok_count, heads_local, HD).astype(jnp.bfloat16)
    key_grad_loc = kv_grad[:, 0].astype(jnp.bfloat16)
    value_grad_loc = kv_grad[:, 1].astype(jnp.bfloat16)
    query_grad, key_grad, value_grad = (
        lax.all_to_all(query_grad_loc, "head", split_axis=0, concat_axis=1, tiled=True),
        lax.all_to_all(key_grad_loc, "head", split_axis=0, concat_axis=1, tiled=True),
        lax.all_to_all(value_grad_loc, "head", split_axis=0, concat_axis=1, tiled=True),
    )
    return (query_grad, key_grad, value_grad)


def solution(mesh):
    placed = (
        P(("seq", "head"), None, None),
        P(("seq", "head"), None, None),
        P(("seq", "head"), None, None),
        P(("seq", "head"), None, None),
        P(("seq", "head"), None, None),
        P(("seq", "head"), None),
        P(),
        P(),
    )
    return jax.shard_map(
        per_device,
        mesh=mesh,
        in_specs=placed,
        out_specs=(
            P(("seq", "head"), None, None),
            P(("seq", "head"), None, None),
            P(("seq", "head"), None, None),
        ),
        check_vma=False,
    )
```

profile of v0, /device:TPU:0, one launch (start us, length us, event | category | flops | bytes accessed | tf_op | source)
XLA Modules:
  0.0 552.0 jit_solution(14091224354696129399)
XLA Ops:
  7.2 4.3 all-to-all-start.4
  27.5 5.6 %all-to-all-done.1 = bf16[288,4,128]{2,0,1:T(8,128)(2,1)S(1)} async-done(((bf16[288,4,128]{2,0,1:T(8,128)(2,1)}), bf16[288,4,128]{2,0,1:T(8,128)(2,1)S(1)}, u32[]{:S(2)}, u32[]{:S(2)}) %all-to-all-start.1) | async-done | bytes 294944 | tf_op jit(solution)/shard_map/all_to_all | solution.py:111
  42.8 4.5 all-to-all-start.3
  49.7 26.2 %all-to-all-done.3 = bf16[288,32,128]{2,0,1:T(8,128)(2,1)} async-done(((bf16[288,32,128]{2,0,1:T(8,128)(2,1)}), bf16[288,32,128]{2,0,1:T(8,128)(2,1)}, u32[]{:S(2)}, u32[]{:S(2)}) %all-to-all-start.3) | async-done | bytes 2359328 | tf_op jit(solution)/shard_map/all_to_all | solution.py:109
  85.6 22.4 %all-to-all-done.5 = bf16[288,32,128]{2,0,1:T(8,128)(2,1)S(1)} async-done(((bf16[288,32,128]{2,0,1:T(8,128)(2,1)}), bf16[288,32,128]{2,0,1:T(8,128)(2,1)S(1)}, u32[]{:S(2)}, u32[]{:S(2)}) %all-to-all-start.5) | async-done | bytes 2359328 | tf_op jit(solution)/shard_map/all_to_all | solution.py:112
  108.0 6.3 %all-to-all-start.2 = ((bf16[8,4,128,2,1,128]{5,3,2,1,4,0:T(2,128)(2,1)}), bf16[8,4,128,2,1,128]{5,3,2,1,4,0:T(2,128)(2,1)}, u32[]{:S(2)}, u32[]{:S(2)}) async-start(bf16[8,4,128,2,1,128]{5,3,2,1,4,0:T(2,128)(2,1)} %copy.262), calls=%async_computation.2 | async-start | bytes 4194304 | tf_op jit(solution)/shard_map/all_to_all | solution.py:167
  119.0 5.4 collective-permute-start
  125.2 4.5 collective-permute-done.1
  130.2 4.0 collective-permute-done
  136.1 70.2 %all-reduce.6.cloned.1.call-done = bf16[2,128,2,128]{3,1,0,2:T(8,128)(2,1)} async-done(((bf16[2,128,2,128]{3,1,0,2:T(8,128)(2,1)}), bf16[2,128,2,128]{3,1,0,2:T(8,128)(2,1)}) %all-reduce.6.cloned.1.call-update) | async-done | bytes 131088 | tf_op jit(solution)/shard_map/psum | solution.py:27
  226.1 6.4 %slice_bitcast_fusion = (bf16[9,8,128,1,128]{4,2,1,3,0:T(8,128)(2,1)}, bf16[9,8,128,1,128]{4,2,1,3,0:T(8,128)(2,1)}) fusion(bf16[9,8,128,2,1,128]{5,2,4,3,1,0:T(8,128)(2,1)} %constant_dynamic-update-slice_fusion.1), kind=kLoop, calls=%fused_computation.51 | loop fusion | bytes 9437184 | tf_op jit(solution)/shard_map/while | solution.py:74
  232.5 122.5 %while.15 = (s32[]{:T(128)}, bf16[9,128,1,8,128]{4,3,1,0,2:T(8,128)(2,1)}, f32[9,8,128,2,1,128]{2,5,1,3,4,0:T(8,128)}, bf16[9,8,128,1,128]{4,2,1,3,0:T(8,128)(2,...) while((s32[]{:T(128)}, ...), condition=%wide.region_4.5_spmd, body=%wide.region_3.4_spmd.sunk | while | flops 1353318400 | bytes 43020592 | solution.py:74
  357.2 4.8 copy.294
  362.0 6.2 %reshape.411 = f32[27,32768]{1,0:T(8,128)} reshape(f32[9,3,128,2,1,128]{5,3,2,1,0,4:T(2,128)} %copy.294) | data formatting | bytes 7077888 | tf_op jit(solution)/shard_map/reshape | solution.py:190
  368.2 5.2 reshape.412
  373.4 4.4 fusion.53
  377.8 4.2 copy.296
  382.0 4.6 all-to-all-start.8
  386.7 9.6 %copy.287 = f32[9,8,128,2,1,128]{5,2,3,0,4,1:T(8,128)} copy(f32[9,8,128,2,1,128]{2,5,1,3,4,0:T(8,128)} %get-tuple-element.93) | data formatting | bytes 18874368 | tf_op jit(solution)/shard_map/while | solution.py:74
  402.7 5.2 collective-permute-start.3
  408.7 74.4 %all-to-all-done.8 = f32[8,4,128,2,1,128]{5,3,2,1,4,0:T(2,128)} async-done(((f32[8,4,128,2,1,128]{5,3,2,1,4,0:T(2,128)}), f32[8,4,128,2,1,128]{5,3,2,1,4,0:T(2,128)}, u32[]{:S(2)}, u32[]{:S(2)}) %all-to-all-start.8) | async-done | bytes 4194336 | tf_op jit(solution)/shard_map/all_to_all | solution.py:199
  488.9 11.4 %fusion.56 = f32[9,128,2,128]{3,0,2,1:T(8,128)S(1)} fusion(f32[8,4,128,2,1,128]{5,3,2,1,4,0:T(2,128)} %all-to-all-done.8, f32[8,4,9]{0,2,1:T(8,128)S(1)} %copy-done.5), kind=kOutput, calls=%fused_computation.58 | convolution fusion | flops 113246208 | bytes 5375104 | tf_op jit(solution)/shard_map/pml,pmbtgd->lbtgd/dot_general | solution.py:202
  501.0 19.8 %all-reduce.8.cloned.1.call-done = f32[2,128,2,1,128]{4,1,3,2,0:T(8,128)} async-done(((f32[2,128,2,1,128]{4,1,3,2,0:T(8,128)}), f32[2,128,2,1,128]{4,1,3,2,0:T(8,128)}) %all-reduce.8.cloned.1.call-update) | async-done | bytes 262160 | tf_op jit(solution)/shard_map/psum | solution.py:177
  529.3 4.7 all-to-all-done.9
  (247 shorter events, 222.6 us)
Async XLA Ops:
  7.2 8.8 %all-to-all-start.4 = ((f32[288,4,8]{0,2,1:T(8,128)}), f32[288,4,8]{0,2,1:T(8,128)S(1)}, u32[]{:S(2)}, u32[]{:S(2)}) async-start(f32[288,4,8]{0,2,1:T(8,128)} %bitcast.356), calls=%async_computation.4 | async-start | bytes 98304 | tf_op jit(solution)/shard_map/all_to_all | solution.py:115
  11.4 7.8 %copy-start.6 = (bf16[288,4,128]{2,1,0:T(4,128)(2,1)S(1)}, bf16[288,4,128]{2,1,0:T(4,128)(2,1)}, u32[]{:S(2)}) copy-start(bf16[288,4,128]{2,1,0:T(4,128)(2,1)} %param.18) | copy-start | bytes 884740
  11.4 15.3 %copy-start.7 = (bf16[288,4,128]{2,1,0:T(4,128)(2,1)S(1)}, bf16[288,4,128]{2,1,0:T(4,128)(2,1)}, u32[]{:S(2)}) copy-start(bf16[288,4,128]{2,1,0:T(4,128)(2,1)} %param.17) | copy-start | bytes 884740
  15.2 21.3 %copy-start.3 = (bf16[288,32,128]{2,1,0:T(8,128)(2,1)S(1)}, bf16[288,32,128]{2,1,0:T(8,128)(2,1)}, u32[]{:S(2)}) copy-start(bf16[288,32,128]{2,1,0:T(8,128)(2,1)} %param.16) | copy-start | bytes 7077892
  15.9 7.3 %all-to-all-start.6 = ((f32[288,4,8]{0,2,1:T(8,128)}), f32[288,4,8]{0,2,1:T(8,128)S(1)}, u32[]{:S(2)}, u32[]{:S(2)}) async-start(f32[288,4,8]{0,2,1:T(8,128)} %bitcast.81), calls=%async_computation.6 | async-start | bytes 98304 | tf_op jit(solution)/shard_map/all_to_all | solution.py:116
  23.3 9.8 %all-to-all-start.1 = ((bf16[288,4,128]{2,0,1:T(8,128)(2,1)}), bf16[288,4,128]{2,0,1:T(8,128)(2,1)S(1)}, u32[]{:S(2)}, u32[]{:S(2)}) async-start(bf16[288,4,128]{2,0,1:T(8,128)(2,1)} %copy.251), calls=%async_computation.1 | async-start | bytes 589824 | tf_op jit(solution)/shard_map/all_to_all | solution.py:111
  33.0 9.8 %all-to-all-start = ((bf16[288,4,128]{2,0,1:T(8,128)(2,1)}), bf16[288,4,128]{2,0,1:T(8,128)(2,1)S(1)}, u32[]{:S(2)}, u32[]{:S(2)}) async-start(bf16[288,4,128]{2,0,1:T(8,128)(2,1)} %copy.250), calls=%async_computation | async-start | bytes 589824 | tf_op jit(solution)/shard_map/all_to_all | solution.py:110
  38.8 8.5 %copy-start.1 = (bf16[288,32,128]{2,1,0:T(8,128)(2,1)S(1)}, bf16[288,32,128]{2,1,0:T(8,128)(2,1)}, u32[]{:S(2)}) copy-start(bf16[288,32,128]{2,1,0:T(8,128)(2,1)} %param.20) | copy-start | bytes 7077892
  42.8 33.1 %all-to-all-start.3 = ((bf16[288,32,128]{2,0,1:T(8,128)(2,1)}), bf16[288,32,128]{2,0,1:T(8,128)(2,1)}, u32[]{:S(2)}, u32[]{:S(2)}) async-start(bf16[288,32,128]{2,0,1:T(8,128)(2,1)} %copy.270), calls=%async_computation.3 | async-start | bytes 4718592 | tf_op jit(solution)/shard_map/all_to_all | solution.py:109
  49.7 29.8 %copy-start.10 = (s32[72,3]{0,1:T(4,128)S(1)}, s32[72,3]{0,1:T(4,128)}, u32[]{:S(2)}) copy-start(s32[72,3]{0,1:T(4,128)} %param.23) | copy-start | bytes 2596
  49.7 30.0 %copy-start.9 = (s32[72,3]{0,1:T(4,128)S(1)}, s32[72,3]{0,1:T(4,128)}, u32[]{:S(2)}) copy-start(s32[72,3]{0,1:T(4,128)} %param.22) | copy-start | bytes 2596
  75.9 32.1 %all-to-all-start.5 = ((bf16[288,32,128]{2,0,1:T(8,128)(2,1)}), bf16[288,32,128]{2,0,1:T(8,128)(2,1)S(1)}, u32[]{:S(2)}, u32[]{:S(2)}) async-start(bf16[288,32,128]{2,0,1:T(8,128)(2,1)} %copy.274), calls=%async_computation.5 | async-start | bytes 4718592 | tf_op jit(solution)/shard_map/all_to_all | solution.py:112
  108.0 110.7 %all-to-all-start.2 = ((bf16[8,4,128,2,1,128]{5,3,2,1,4,0:T(2,128)(2,1)}), bf16[8,4,128,2,1,128]{5,3,2,1,4,0:T(2,128)(2,1)}, u32[]{:S(2)}, u32[]{:S(2)}) async-start(bf16[8,4,128,2,1,128]{5,3,2,1,4,0:T(2,128)(2,1)} %copy.262), calls=%async_computation.2 | async-start | bytes 4194304 | tf_op jit(solution)/shard_map/all_to_all | solution.py:167
  114.2 92.0 %all-reduce.6.cloned.1.call-start = ((), (), s32[]{:S(2)}) async-start(), calls=%async_computation.11 | async-start | bytes 262144 | tf_op jit(solution)/shard_map/psum | solution.py:27
  117.7 11.9 %collective-permute-start.1 = (bf16[128,2,1,128]{3,0,2,1:T(8,128)(2,1)S(1)}, bf16[128,2,1,128]{3,0,2,1:T(8,128)(2,1)S(1)}, u32[]{:S(2)}, u32[]{:S(2)}) collective-permute-start(bf16[128,2,1,128]{3,0,2,1:T(8,128)(2,1)S(1)} %get-tuple-element.196), channel_id=1, source_target_pairs={{4,0},{8,4},{12,8},{16,12},{20,16},{24,20},{28,24},{5,1},{9,5},{13... | collective-permute-start | bytes 196616 | tf_op jit(solution)/shard_map/ppermute | solution.py:20
  119.0 15.2 %collective-permute-start = (bf16[128,2,1,128]{3,0,2,1:T(8,128)(2,1)S(1)}, bf16[128,2,1,128]{3,0,2,1:T(8,128)(2,1)}, u32[]{:S(2)}, u32[]{:S(2)}) collective-permute-start(bf16[128,2,1,128]{3,0,2,1:T(8,128)(2,1)S(1)} %get-tuple-element.197), channel_id=1, source_target_pairs={{0,4},{4,8},{8,12},{12,16},{16,20},{20,24},{24,28},{1,5},{5,9},{9,... | collective-permute-start | bytes 196616 | tf_op jit(solution)/shard_map/ppermute | solution.py:19
  368.2 5.2 copy-start.11
  382.0 101.1 %all-to-all-start.8 = ((f32[8,4,128,2,1,128]{5,3,2,1,4,0:T(2,128)}), f32[8,4,128,2,1,128]{5,3,2,1,4,0:T(2,128)}, u32[]{:S(2)}, u32[]{:S(2)}) async-start(f32[8,4,128,2,1,128]{5,3,2,1,4,0:T(2,128)} %copy.296), calls=%async_computation.8 | async-start | bytes 8388608 | tf_op jit(solution)/shard_map/all_to_all | solution.py:199
  386.6 134.2 %all-reduce.8.cloned.1.call-start = ((), (), s32[]{:S(2)}) async-start(), calls=%async_computation.12 | async-start | bytes 524288 | tf_op jit(solution)/shard_map/psum | solution.py:177
  399.5 87.5 %collective-permute-start.2 = (bf16[128,2,1,128]{3,0,1,2:T(8,128)(2,1)}, bf16[128,2,1,128]{3,0,1,2:T(8,128)(2,1)}, u32[]{:S(2)}, u32[]{:S(2)}) collective-permute-start(bf16[128,2,1,128]{3,0,1,2:T(8,128)(2,1)} %get-tuple-element.191), channel_id=1, source_target_pairs={{4,0},{8,4},{12,8},{16,12},{20,16},{24,20},{28,24},{5,1},{9,5},{13... | collective-permute-start | bytes 196616 | tf_op jit(solution)/shard_map/ppermute | solution.py:33
  402.7 85.3 %collective-permute-start.3 = (bf16[128,2,1,128]{3,0,1,2:T(8,128)(2,1)}, bf16[128,2,1,128]{3,0,1,2:T(8,128)(2,1)}, u32[]{:S(2)}, u32[]{:S(2)}) collective-permute-start(bf16[128,2,1,128]{3,0,1,2:T(8,128)(2,1)} %get-tuple-element.190), channel_id=1, source_target_pairs={{0,4},{4,8},{8,12},{12,16},{16,20},{20,24},{24,28},{1,5},{5,9},{9,... | collective-permute-start | bytes 196616 | tf_op jit(solution)/shard_map/ppermute | solution.py:33
  483.2 41.0 %all-to-all-start.7 = ((bf16[1152,8,128]{2,1,0:T(8,128)(2,1)}), bf16[1152,8,128]{2,1,0:T(8,128)(2,1)S(1)}, u32[]{:S(2)}, u32[]{:S(2)}) async-start(bf16[1152,8,128]{2,1,0:T(8,128)(2,1)} %bitcast.342), calls=%async_computation.7 | async-start | bytes 4718592 | tf_op jit(solution)/shard_map/all_to_all | solution.py:216
  524.2 9.8 %all-to-all-start.9 = ((bf16[4,2,18432]{2,1,0:T(2,128)(2,1)}), bf16[4,2,18432]{2,1,0:T(2,128)(2,1)S(1)}, u32[]{:S(2)}, u32[]{:S(2)}) async-start(bf16[4,2,18432]{2,1,0:T(2,128)(2,1)} %reshape.453), calls=%async_computation.9 | async-start | bytes 589824 | tf_op jit(solution)/shard_map/all_to_all | solution.py:217
  534.0 9.8 %all-to-all-start.10 = ((bf16[4,2,18432]{2,1,0:T(2,128)(2,1)}), bf16[4,2,18432]{2,1,0:T(2,128)(2,1)S(1)}, u32[]{:S(2)}, u32[]{:S(2)}) async-start(bf16[4,2,18432]{2,1,0:T(2,128)(2,1)} %reshape.455), calls=%async_computation.10 | async-start | bytes 589824 | tf_op jit(solution)/shard_map/all_to_all | solution.py:218
  (13 other events, 37.7 us)
Sparse Core Ops, SparseCore 0:
  125.3 80.9 all-reduce.5
  408.9 111.9 all-reduce.7
where the time goes:
time: 562 us; the launch traced here: 552 us
  waiting for transfers between devices  242 us (43%)
  local copies, waits for them, and re-layouts  109 us (19%)
  matrix products  103 us (18%)
  starting transfers between devices  57.4 us (10%)
  other arithmetic  25.4 us (5%)
  between operations  14.7 us (3%)
    all_to_all x1, waiting for transfers between devices, per_device(): lax.all_to_all(returning, 'seq', split_axis=0, concat_axis=0, tiled=True)  74.4 us
    psum x1, waiting for transfers between devices, broadcast(): return lax.psum(kept, axis)  70.2 us
    dot_general x9, matrix products, block_grads(): jnp.einsum('mghij,ighd->mjgd', weights_rounded, grad_block, preferred_ele...  29.3 us
    all_to_all x1, waiting for transfers between devices, per_device(): lax.all_to_all(queries, 'head', split_axis=1, concat_axis=0, tiled=True)  26.2 us
    all_to_all x1, waiting for transfers between devices, per_device(): lax.all_to_all(output_grad, 'head', split_axis=1, concat_axis=0, tiled=True)  22.4 us
    dot_general x9, matrix products, block_grads(): jnp.einsum('ighd,mjgd->mghij', grad_block, value_blocks, preferred_elemen...  21.9 us
    psum x1, waiting for transfers between devices, per_device(): global_total = lax.psum(global_part, 'seq')  19.8 us
    dynamic_slice x18, local copies, waits for them, and re-layouts, local_grads(): lax.map(single_block, (query_split, grad_split, logsum_split, delta_split...  17.3 us
  transfers between devices with their start and end apart: 17, of which 12 were waited for; matrix products, arithmetic and copies ran while one was open for 13% of the time, Pallas kernels for 0%

commit v1 on v0

--- a/solution.py
+++ b/solution.py
@@ -24,7 +24,7 @@
 
 def broadcast(value, axis, source):
     kept = jnp.where(lax.axis_index(axis) == source, value, 0).astype(value.dtype)
-    return lax.psum(kept, axis)
+    return jnp.sum(lax.all_gather(kept, axis), axis=0)
 
 
 def from_behind(value, axis, steps):

time: 562 us -> 532 us (0.947)
  waiting for transfers between devices: 242 us -> 204 us
  starting transfers between devices: 57.4 us -> 66.8 us
    psum x1 -> x0, waiting for transfers between devices: 70.2 us -> none  [broadcast(): return lax.psum(kept, axis)]
    all_gather x0 -> x1, waiting for transfers between devices: none -> 31.2 us  [broadcast(): return jnp.sum(lax.all_gather(kept, axis), axis=0)]
    all_to_all x1, starting transfers between devices: 4.57 us -> 13.7 us  [per_device(): lax.all_to_all(returning, 'seq', split_axis=0, concat_axis=0, tiled=True)]
    unnamed x40 -> x42, local copies, waits for them, and re-layouts: 16.3 us -> 14.3 us
  transfers between devices with their start and end apart: 17 -> 17, of which waited for: 12 -> 12; matrix products, arithmetic and copies ran while one was open for 13% -> 14% of each run, Pallas kernels for 0% -> 0%
where the time goes in v1:
time: 532 us; the launch traced here: 522 us
  waiting for transfers between devices  204 us (38%)
  local copies, waits for them, and re-layouts  106 us (20%)
  matrix products  103 us (19%)
  starting transfers between devices  66.8 us (13%)
  other arithmetic  26.7 us (5%)
  between operations  14.8 us (3%)
    all_to_all x1, waiting for transfers between devices, per_device(): lax.all_to_all(returning, 'seq', split_axis=0, concat_axis=0, tiled=True)  76.9 us
    all_gather x1, waiting for transfers between devices, broadcast(): return jnp.sum(lax.all_gather(kept, axis), axis=0)  31.2 us
    dot_general x9, matrix products, block_grads(): jnp.einsum('mghij,ighd->mjgd', weights_rounded, grad_block, preferred_ele...  29.3 us
    all_to_all x1, waiting for transfers between devices, per_device(): lax.all_to_all(queries, 'head', split_axis=1, concat_axis=0, tiled=True)  26.2 us
    all_to_all x1, waiting for transfers between devices, per_device(): lax.all_to_all(output_grad, 'head', split_axis=1, concat_axis=0, tiled=True)  22.4 us
    dot_general x9, matrix products, block_grads(): jnp.einsum('ighd,mjgd->mghij', grad_block, value_blocks, preferred_elemen...  21.9 us
    psum x1, waiting for transfers between devices, per_device(): global_total = lax.psum(global_part, 'seq')  18 us
    dynamic_slice x18, local copies, waits for them, and re-layouts, local_grads(): lax.map(single_block, (query_split, grad_split, logsum_split, delta_split...  17.3 us
  transfers between devices with their start and end apart: 17, of which 12 were waited for; matrix products, arithmetic and copies ran while one was open for 14% of the time, Pallas kernels for 0%

profile of v1, /device:TPU:0, one launch (start us, length us, event | category | flops | bytes accessed | tf_op | source)
XLA Modules:
  0.0 522.3 jit_solution(8715865567757599468)
XLA Ops:
  7.2 4.3 all-to-all-start.4
  27.5 5.6 %all-to-all-done.1 = bf16[288,4,128]{2,0,1:T(8,128)(2,1)S(1)} async-done(((bf16[288,4,128]{2,0,1:T(8,128)(2,1)}), bf16[288,4,128]{2,0,1:T(8,128)(2,1)S(1)}, u32[]{:S(2)}, u32[]{:S(2)}) %all-to-all-start.1) | async-done | bytes 294944 | tf_op jit(solution)/shard_map/all_to_all | solution.py:111
  38.8 4.0 all-to-all-done
  42.8 4.5 all-to-all-start.3
  49.7 26.2 %all-to-all-done.3 = bf16[288,32,128]{2,0,1:T(8,128)(2,1)} async-done(((bf16[288,32,128]{2,0,1:T(8,128)(2,1)}), bf16[288,32,128]{2,0,1:T(8,128)(2,1)}, u32[]{:S(2)}, u32[]{:S(2)}) %all-to-all-start.3) | async-done | bytes 2359328 | tf_op jit(solution)/shard_map/all_to_all | solution.py:109
  85.6 22.4 %all-to-all-done.5 = bf16[288,32,128]{2,0,1:T(8,128)(2,1)S(1)} async-done(((bf16[288,32,128]{2,0,1:T(8,128)(2,1)}), bf16[288,32,128]{2,0,1:T(8,128)(2,1)S(1)}, u32[]{:S(2)}, u32[]{:S(2)}) %all-to-all-start.5) | async-done | bytes 2359328 | tf_op jit(solution)/shard_map/all_to_all | solution.py:112
  107.9 6.3 %all-to-all-start.2 = ((bf16[8,4,128,2,1,128]{5,3,2,1,4,0:T(2,128)(2,1)}), bf16[8,4,128,2,1,128]{5,3,2,1,4,0:T(2,128)(2,1)}, u32[]{:S(2)}, u32[]{:S(2)}) async-start(bf16[8,4,128,2,1,128]{5,3,2,1,4,0:T(2,128)(2,1)} %copy.261), calls=%async_computation.2 | async-start | bytes 4194304 | tf_op jit(solution)/shard_map/all_to_all | solution.py:167
  118.2 5.6 %collective-permute-start = (bf16[128,2,1,128]{3,0,2,1:T(8,128)(2,1)S(1)}, bf16[128,2,1,128]{3,0,2,1:T(8,128)(2,1)}, u32[]{:S(2)}, u32[]{:S(2)}) collective-permute-start(bf16[128,2,1,128]{3,0,2,1:T(8,128)(2,1)S(1)} %get-tuple-element.197), channel_id=1, source_target_pairs={{0,4},{4,8},{8,12},{12,16},{16,20},{20,24},{24,28},{1,5},{5,9},{9,... | collective-permute-start | bytes 196616 | tf_op jit(solution)/shard_map/ppermute | solution.py:19
  125.3 5.5 %collective-permute-done.1 = bf16[128,2,1,128]{3,0,2,1:T(8,128)(2,1)S(1)} collective-permute-done((bf16[128,2,1,128]{3,0,2,1:T(8,128)(2,1)S(1)}, bf16[128,2,1,128]{3,0,2,1:T(8,128)(2,1)S(1)}, u32[]{:S(2)}, u32[]{:S(2)}) %collective-permute-start.1) | collective-permute-done | bytes 65568 | tf_op jit(solution)/shard_map/ppermute | solution.py:20
  142.8 31.2 %all-gather.3.cloned.1.call-done = bf16[2048,2,1,128]{3,0,2,1:T(8,128)(2,1)} async-done(((bf16[256,2,1,128]{3,0,2,1:T(8,128)(2,1)}), bf16[2048,2,1,128]{3,0,2,1:T(8,128)(2,1)}) %all-gather.3.cloned.1.call-update) | async-done | bytes 1048592 | tf_op jit(solution)/shard_map/all_gather | solution.py:27
  187.0 6.4 %slice_bitcast_fusion = (bf16[9,8,128,1,128]{4,2,1,3,0:T(8,128)(2,1)}, bf16[9,8,128,1,128]{4,2,1,3,0:T(8,128)(2,1)}) fusion(bf16[9,8,128,2,1,128]{5,2,4,3,1,0:T(8,128)(2,1)} %constant_dynamic-update-slice_fusion.1), kind=kLoop, calls=%fused_computation.51 | loop fusion | bytes 9437184 | tf_op jit(solution)/shard_map/while | solution.py:74
  193.4 122.4 %while.15 = (s32[]{:T(128)}, bf16[9,128,1,8,128]{4,3,1,0,2:T(8,128)(2,1)}, f32[9,8,128,2,1,128]{2,5,1,3,4,0:T(8,128)}, bf16[9,8,128,1,128]{4,2,1,3,0:T(8,128)(2,...) while((s32[]{:T(128)}, ...), condition=%wide.region_4.5_spmd, body=%wide.region_3.4_spmd.sunk | while | flops 1353318400 | bytes 43020592 | solution.py:74
  318.1 4.7 copy.293
  322.8 6.2 %reshape.413 = f32[27,32768]{1,0:T(8,128)} reshape(f32[9,3,128,2,1,128]{5,3,2,1,0,4:T(2,128)} %copy.293) | data formatting | bytes 7077888 | tf_op jit(solution)/shard_map/reshape | solution.py:190
  329.0 4.9 reshape.414
  333.9 4.4 fusion.53
  338.3 4.2 copy.295
  342.5 13.7 %all-to-all-start.8 = ((f32[8,4,128,2,1,128]{5,3,2,1,4,0:T(2,128)}), f32[8,4,128,2,1,128]{5,3,2,1,4,0:T(2,128)}, u32[]{:S(2)}, u32[]{:S(2)}) async-start(f32[8,4,128,2,1,128]{5,3,2,1,4,0:T(2,128)} %copy.295), calls=%async_computation.8 | async-start | bytes 8388608 | tf_op jit(solution)/shard_map/all_to_all | solution.py:199
  356.3 9.6 %copy.286 = f32[9,8,128,2,1,128]{5,2,3,0,4,1:T(8,128)} copy(f32[9,8,128,2,1,128]{2,5,1,3,4,0:T(8,128)} %get-tuple-element.93) | data formatting | bytes 18874368 | tf_op jit(solution)/shard_map/while | solution.py:74
  372.3 5.2 collective-permute-start.3
  378.4 76.9 %all-to-all-done.8 = f32[8,4,128,2,1,128]{5,3,2,1,4,0:T(2,128)} async-done(((f32[8,4,128,2,1,128]{5,3,2,1,4,0:T(2,128)}), f32[8,4,128,2,1,128]{5,3,2,1,4,0:T(2,128)}, u32[]{:S(2)}, u32[]{:S(2)}) %all-to-all-start.8) | async-done | bytes 4194336 | tf_op jit(solution)/shard_map/all_to_all | solution.py:199
  461.0 11.4 %fusion.56 = f32[9,128,2,128]{3,0,2,1:T(8,128)S(1)} fusion(f32[8,4,128,2,1,128]{5,3,2,1,4,0:T(2,128)} %all-to-all-done.8, f32[8,4,9]{0,2,1:T(8,128)S(1)} %copy-done.6), kind=kOutput, calls=%fused_computation.58 | convolution fusion | flops 113246208 | bytes 5375104 | tf_op jit(solution)/shard_map/pml,pmbtgd->lbtgd/dot_general | solution.py:202
  473.1 18.0 %all-reduce.5.cloned.1.call-done = f32[2,128,2,1,128]{4,1,3,2,0:T(8,128)} async-done(((f32[2,128,2,1,128]{4,1,3,2,0:T(8,128)}), f32[2,128,2,1,128]{4,1,3,2,0:T(8,128)}) %all-reduce.5.cloned.1.call-update) | async-done | bytes 262160 | tf_op jit(solution)/shard_map/psum | solution.py:177
  499.6 4.7 all-to-all-done.9
  (250 shorter events, 221.2 us)
Async XLA Ops:
  7.2 8.8 %all-to-all-start.4 = ((f32[288,4,8]{0,2,1:T(8,128)}), f32[288,4,8]{0,2,1:T(8,128)S(1)}, u32[]{:S(2)}, u32[]{:S(2)}) async-start(f32[288,4,8]{0,2,1:T(8,128)} %bitcast.358), calls=%async_computation.4 | async-start | bytes 98304 | tf_op jit(solution)/shard_map/all_to_all | solution.py:115
  11.4 7.8 %copy-start.7 = (bf16[288,4,128]{2,1,0:T(4,128)(2,1)S(1)}, bf16[288,4,128]{2,1,0:T(4,128)(2,1)}, u32[]{:S(2)}) copy-start(bf16[288,4,128]{2,1,0:T(4,128)(2,1)} %param.18) | copy-start | bytes 884740
  11.4 15.3 %copy-start.8 = (bf16[288,4,128]{2,1,0:T(4,128)(2,1)S(1)}, bf16[288,4,128]{2,1,0:T(4,128)(2,1)}, u32[]{:S(2)}) copy-start(bf16[288,4,128]{2,1,0:T(4,128)(2,1)} %param.17) | copy-start | bytes 884740
  15.2 21.3 %copy-start.3 = (bf16[288,32,128]{2,1,0:T(8,128)(2,1)S(1)}, bf16[288,32,128]{2,1,0:T(8,128)(2,1)}, u32[]{:S(2)}) copy-start(bf16[288,32,128]{2,1,0:T(8,128)(2,1)} %param.16) | copy-start | bytes 7077892
  15.9 7.3 %all-to-all-start.6 = ((f32[288,4,8]{0,2,1:T(8,128)}), f32[288,4,8]{0,2,1:T(8,128)S(1)}, u32[]{:S(2)}, u32[]{:S(2)}) async-start(f32[288,4,8]{0,2,1:T(8,128)} %bitcast.82), calls=%async_computation.6 | async-start | bytes 98304 | tf_op jit(solution)/shard_map/all_to_all | solution.py:116
  23.3 9.8 %all-to-all-start.1 = ((bf16[288,4,128]{2,0,1:T(8,128)(2,1)}), bf16[288,4,128]{2,0,1:T(8,128)(2,1)S(1)}, u32[]{:S(2)}, u32[]{:S(2)}) async-start(bf16[288,4,128]{2,0,1:T(8,128)(2,1)} %copy.250), calls=%async_computation.1 | async-start | bytes 589824 | tf_op jit(solution)/shard_map/all_to_all | solution.py:111
  33.0 9.8 %all-to-all-start = ((bf16[288,4,128]{2,0,1:T(8,128)(2,1)}), bf16[288,4,128]{2,0,1:T(8,128)(2,1)S(1)}, u32[]{:S(2)}, u32[]{:S(2)}) async-start(bf16[288,4,128]{2,0,1:T(8,128)(2,1)} %copy.249), calls=%async_computation | async-start | bytes 589824 | tf_op jit(solution)/shard_map/all_to_all | solution.py:110
  38.8 8.5 %copy-start.1 = (bf16[288,32,128]{2,1,0:T(8,128)(2,1)S(1)}, bf16[288,32,128]{2,1,0:T(8,128)(2,1)}, u32[]{:S(2)}) copy-start(bf16[288,32,128]{2,1,0:T(8,128)(2,1)} %param.20) | copy-start | bytes 7077892
  42.8 33.0 %all-to-all-start.3 = ((bf16[288,32,128]{2,0,1:T(8,128)(2,1)}), bf16[288,32,128]{2,0,1:T(8,128)(2,1)}, u32[]{:S(2)}, u32[]{:S(2)}) async-start(bf16[288,32,128]{2,0,1:T(8,128)(2,1)} %copy.269), calls=%async_computation.3 | async-start | bytes 4718592 | tf_op jit(solution)/shard_map/all_to_all | solution.py:109
  49.7 29.8 %copy-start.11 = (s32[72,3]{0,1:T(4,128)S(1)}, s32[72,3]{0,1:T(4,128)}, u32[]{:S(2)}) copy-start(s32[72,3]{0,1:T(4,128)} %param.23) | copy-start | bytes 2596
  49.7 30.0 %copy-start.10 = (s32[72,3]{0,1:T(4,128)S(1)}, s32[72,3]{0,1:T(4,128)}, u32[]{:S(2)}) copy-start(s32[72,3]{0,1:T(4,128)} %param.22) | copy-start | bytes 2596
  75.9 32.1 %all-to-all-start.5 = ((bf16[288,32,128]{2,0,1:T(8,128)(2,1)}), bf16[288,32,128]{2,0,1:T(8,128)(2,1)S(1)}, u32[]{:S(2)}, u32[]{:S(2)}) async-start(bf16[288,32,128]{2,0,1:T(8,128)(2,1)} %copy.273), calls=%async_computation.5 | async-start | bytes 4718592 | tf_op jit(solution)/shard_map/all_to_all | solution.py:112
  107.9 71.6 %all-to-all-start.2 = ((bf16[8,4,128,2,1,128]{5,3,2,1,4,0:T(2,128)(2,1)}), bf16[8,4,128,2,1,128]{5,3,2,1,4,0:T(2,128)(2,1)}, u32[]{:S(2)}, u32[]{:S(2)}) async-start(bf16[8,4,128,2,1,128]{5,3,2,1,4,0:T(2,128)(2,1)} %copy.261), calls=%async_computation.2 | async-start | bytes 4194304 | tf_op jit(solution)/shard_map/all_to_all | solution.py:167
  114.2 59.8 %all-gather.3.cloned.1.call-start = ((), (), s32[]{:S(2)}) async-start(), calls=%async_computation.12 | async-start | bytes 1179648 | tf_op jit(solution)/shard_map/all_gather | solution.py:27
  116.9 13.9 %collective-permute-start.1 = (bf16[128,2,1,128]{3,0,2,1:T(8,128)(2,1)S(1)}, bf16[128,2,1,128]{3,0,2,1:T(8,128)(2,1)S(1)}, u32[]{:S(2)}, u32[]{:S(2)}) collective-permute-start(bf16[128,2,1,128]{3,0,2,1:T(8,128)(2,1)S(1)} %get-tuple-element.196), channel_id=1, source_target_pairs={{4,0},{8,4},{12,8},{16,12},{20,16},{24,20},{28,24},{5,1},{9,5},{13... | collective-permute-start | bytes 196616 | tf_op jit(solution)/shard_map/ppermute | solution.py:20
  118.2 16.6 %collective-permute-start = (bf16[128,2,1,128]{3,0,2,1:T(8,128)(2,1)S(1)}, bf16[128,2,1,128]{3,0,2,1:T(8,128)(2,1)}, u32[]{:S(2)}, u32[]{:S(2)}) collective-permute-start(bf16[128,2,1,128]{3,0,2,1:T(8,128)(2,1)S(1)} %get-tuple-element.197), channel_id=1, source_target_pairs={{0,4},{4,8},{8,12},{12,16},{16,20},{20,24},{24,28},{1,5},{5,9},{9,... | collective-permute-start | bytes 196616 | tf_op jit(solution)/shard_map/ppermute | solution.py:19
  142.8 33.9 %copy-start.4 = (bf16[1152,2,1,128]{3,0,2,1:T(8,128)(2,1)S(1)}, bf16[1152,2,1,128]{3,0,2,1:T(8,128)(2,1)}, u32[]{:S(2)}) copy-start(bf16[1152,2,1,128]{3,0,2,1:T(8,128)(2,1)} %get-tuple-element.195) | copy-start | bytes 1769476
  342.5 112.7 %all-to-all-start.8 = ((f32[8,4,128,2,1,128]{5,3,2,1,4,0:T(2,128)}), f32[8,4,128,2,1,128]{5,3,2,1,4,0:T(2,128)}, u32[]{:S(2)}, u32[]{:S(2)}) async-start(f32[8,4,128,2,1,128]{5,3,2,1,4,0:T(2,128)} %copy.295), calls=%async_computation.8 | async-start | bytes 8388608 | tf_op jit(solution)/shard_map/all_to_all | solution.py:199
  356.3 134.8 %all-reduce.5.cloned.1.call-start = ((), (), s32[]{:S(2)}) async-start(), calls=%async_computation.11 | async-start | bytes 524288 | tf_op jit(solution)/shard_map/psum | solution.py:177
  369.1 90.0 %collective-permute-start.2 = (bf16[128,2,1,128]{3,0,1,2:T(8,128)(2,1)}, bf16[128,2,1,128]{3,0,1,2:T(8,128)(2,1)}, u32[]{:S(2)}, u32[]{:S(2)}) collective-permute-start(bf16[128,2,1,128]{3,0,1,2:T(8,128)(2,1)} %get-tuple-element.191), channel_id=1, source_target_pairs={{4,0},{8,4},{12,8},{16,12},{20,16},{24,20},{28,24},{5,1},{9,5},{13... | collective-permute-start | bytes 196616 | tf_op jit(solution)/shard_map/ppermute | solution.py:33
  372.3 87.8 %collective-permute-start.3 = (bf16[128,2,1,128]{3,0,1,2:T(8,128)(2,1)}, bf16[128,2,1,128]{3,0,1,2:T(8,128)(2,1)}, u32[]{:S(2)}, u32[]{:S(2)}) collective-permute-start(bf16[128,2,1,128]{3,0,1,2:T(8,128)(2,1)} %get-tuple-element.190), channel_id=1, source_target_pairs={{0,4},{4,8},{8,12},{12,16},{16,20},{20,24},{24,28},{1,5},{5,9},{9,... | collective-permute-start | bytes 196616 | tf_op jit(solution)/shard_map/ppermute | solution.py:33
  455.2 39.2 %all-to-all-start.7 = ((bf16[1152,8,128]{2,1,0:T(8,128)(2,1)}), bf16[1152,8,128]{2,1,0:T(8,128)(2,1)S(1)}, u32[]{:S(2)}, u32[]{:S(2)}) async-start(bf16[1152,8,128]{2,1,0:T(8,128)(2,1)} %bitcast.343), calls=%async_computation.7 | async-start | bytes 4718592 | tf_op jit(solution)/shard_map/all_to_all | solution.py:216
  494.5 9.8 %all-to-all-start.9 = ((bf16[4,2,18432]{2,1,0:T(2,128)(2,1)}), bf16[4,2,18432]{2,1,0:T(2,128)(2,1)S(1)}, u32[]{:S(2)}, u32[]{:S(2)}) async-start(bf16[4,2,18432]{2,1,0:T(2,128)(2,1)} %reshape.457), calls=%async_computation.9 | async-start | bytes 589824 | tf_op jit(solution)/shard_map/all_to_all | solution.py:217
  504.3 9.8 %all-to-all-start.10 = ((bf16[4,2,18432]{2,1,0:T(2,128)(2,1)}), bf16[4,2,18432]{2,1,0:T(2,128)(2,1)S(1)}, u32[]{:S(2)}, u32[]{:S(2)}) async-start(bf16[4,2,18432]{2,1,0:T(2,128)(2,1)} %reshape.459), calls=%async_computation.10 | async-start | bytes 589824 | tf_op jit(solution)/shard_map/all_to_all | solution.py:218
  (14 other events, 42.6 us)
Sparse Core Ops, SparseCore 0:
  117.8 56.2 all-gather.2
  378.5 112.5 all-reduce.4
